TPU v7x, 256 devices: a whole 4x4x8 slice. The times are simulated.
256 devices in a mesh: depth: 64 (over y, z, core), xr: 4 (over x).
Axes of the slice: x: 4, y: 4, z: 8, core: 2. Of those that a mesh axis runs over, the one named last changes fastest.
Arguments:
- sound_field: float32 [2, 4096, 3584], P(None, 'depth', 'xr'), may hold values from -6 to 6
- index_start: float32 [4096, 3584], P('depth', 'xr'), may hold values from 0.8 to 0.98
- index_end: float32 [4096, 3584], P('depth', 'xr'), may hold values from 0.8 to 0.98
Outputs:
- stepped: float32 [2, 4096, 3584], P(None, ('depth', 'xr'))
All inputs are finite; a program needn't handle non-finite values.
Results may differ from a plain program's by a relative error of at most 0.00035.
Values sent between devices are 32-bit elements; how exact they have to be, the bound alone decides.
No kernel may reach another device: no remote copies, remote signals or barrier semaphores. Data moves between devices by JAX's collectives and lax.ppermute only.
A program may use at most 128 MiB of HBM per device.

v0:
```python
import jax
import jax.numpy as jnp
from jax import lax
from jax.experimental import pallas as pl
from jax.experimental.pallas import tpu as pltpu
from jax.sharding import Mesh
from jax.sharding import PartitionSpec as P

DEPTH = ("y", "z", "c")

DEPTH_STIFFNESS = 1.6
CROSS_STIFFNESS = 1.2
NUMER = complex(2.857, 0.004)
DENOM = complex(2.857, -0.004)

MIX = (NUMER / DENOM) ** 2

SUB = 8
LANE = 128
CELLS = 64
PARTS = 12


def constants(stiffness):
    slope = -0.5 / stiffness
    base = 2.0 - (1.0 / DENOM).real / stiffness - slope
    swing = -(1.0 / DENOM).imag / stiffness
    push = ((DENOM - NUMER) / (NUMER * DENOM * stiffness)).imag
    return base, slope, swing, push


def mul(a, b):
    return a[0] * b[0] - a[1] * b[1], a[0] * b[1] + a[1] * b[0]


def add(a, b):
    return a[0] + b[0], a[1] + b[1]


def sub(a, b):
    return a[0] - b[0], a[1] - b[1]


def scaled(a, s):
    return a[0] * s, a[1] * s


def pick(flag, yes, no):
    return [(jnp.where(flag, p[0], q[0]), jnp.where(flag, p[1], q[1])) for p, q in zip(yes, no)]


def compose(early, late):
    a00, a10, a01, a11, r0, r1 = early
    b00, b10, b01, b11, s0, s1 = late
    return [
        add(mul(b00, a00), mul(b01, a10)),
        add(mul(b10, a00), mul(b11, a10)),
        add(mul(b00, a01), mul(b01, a11)),
        add(mul(b10, a01), mul(b11, a11)),
        add(r0, add(mul(a00, s0), mul(a10, s1))),
        add(r1, add(mul(a01, s0), mul(a11, s1))),
    ]


def normal(state):
    f0, f1, g = state
    size = jnp.maximum(
        jnp.maximum(jnp.abs(f0[0]), jnp.abs(f0[1])), jnp.maximum(jnp.abs(f1[0]), jnp.abs(f1[1]))
    )
    scale = 1.0 / size
    return [scaled(f0, scale), scaled(f1, scale), scaled(g, scale)]


def advance(state, span):
    f0, f1, g = state
    t00, t10, t01, t11, s0, s1 = span
    return [
        add(mul(t00, f0), mul(t01, f1)),
        add(mul(t10, f0), mul(t11, f1)),
        add(g, add(mul(f0, s0), mul(f1, s1))),
    ]


def retreat(state, span):
    p0, p1, h = state
    t00, t10, t01, t11, s0, s1 = span
    q0 = sub(mul(t11, p0), mul(t01, p1))
    q1 = sub(mul(t00, p1), mul(t10, p0))
    return [q0, q1, add(h, add(mul(q0, s0), mul(q1, s1)))]


def meet(left, right):
    f0, f1, g = left
    p0, p1, h = right
    det = sub(mul(f1, p0), mul(f0, p1))
    scale = -1.0 / (det[0] * det[0] + det[1] * det[1])
    inverse = (det[0] * scale, -det[1] * scale)
    v0 = mul(add(mul(f0, h), mul(p0, g)), inverse)
    v1 = mul(add(mul(g, p1), mul(f1, h)), inverse)
    return v0, v1


def ends(like):
    zero = jnp.zeros_like(like)
    one = zero + 1.0
    return [(zero, zero), (one, zero), (zero, zero)], [(one, zero), (zero, zero), (zero, zero)]


SPREAD = 7


def read(ref):
    values = [ref[SUB * i : SUB * (i + 1), :] for i in range(9)] + [ref[pl.ds(SPREAD, SUB, stride=SUB), :]]
    t00, t10, along, s0, s1 = zip(values[0::2], values[1::2])
    scale = 1.0 / (t00[0] * t00[0] + t00[1] * t00[1] + t10[0] * t10[0] + t10[1] * t10[1])
    p, q = mul(along, t00), mul(along, t10)
    t01 = (p[0] - t10[0] * scale, p[1] + t10[1] * scale)
    t11 = (q[0] + t00[0] * scale, q[1] - t00[1] * scale)
    return [t00, t10, t01, t11, s0, s1]


def write(ref, span):
    t00, t10, t01, t11, s0, s1 = span
    scale = 1.0 / (t00[0] * t00[0] + t00[1] * t00[1] + t10[0] * t10[0] + t10[1] * t10[1])
    along = add(mul((t00[0], -t00[1]), t01), mul((t10[0], -t10[1]), t11))
    values = [*t00, *t10, *scaled(along, scale), *s0, *s1]
    for i in range(9):
        ref[SUB * i : SUB * (i + 1), :] = values[i]
    ref[pl.ds(SPREAD, SPREAD, stride=SUB), :] = values[9][:SPREAD]


def rows(k):
    return pl.ds(SUB * k, SUB)


def step(c, swing, now, past, u=None):
    if u is not None:
        past = sub(past, u)
    return (c * now[0] - (swing * now[1] + past[0]), c * now[1] + (swing * now[0] - past[1]))


def start_pair():
    zero = jnp.zeros((SUB, LANE), jnp.float32)
    one = zero + 1.0
    return [[(one, zero), (zero, zero)], [(zero, zero), (one, zero)]]


def still():
    zero = jnp.zeros((SUB, LANE), jnp.float32)
    return [(zero, zero), (zero, zero)]


def through(matrix, v0, v1):
    t00, t10, t01, t11 = matrix
    return add(mul(t00, v0), mul(t01, v1)), add(mul(t10, v0), mul(t11, v1))


def product(late, early):
    first = through(late, early[0], early[1])
    second = through(late, early[2], early[3])
    return [first[0], first[1], second[0], second[1]]


def sums_of(matrix, p0, p1):
    t00, t10, t01, t11 = matrix
    return sub(mul(t00, p1), mul(t10, p0)), sub(mul(t01, p1), mul(t11, p0))


def read_all(ref, first, count):
    return [(ref[first + 2 * i], ref[first + 2 * i + 1]) for i in range(count)]


def write_all(ref, first, parts):
    for i, part in enumerate(parts):
        ref[first + 2 * i] = part[0]
        ref[first + 2 * i + 1] = part[1]


def open_kernel(field, start, end, own, snap, source, curve, end_in, field_in, start_in, sems):
    base, slope, swing, _ = constants(DEPTH_STIFFNESS)
    piece = CELLS // 4
    loads = []
    for i in range(4):
        some = pl.ds(piece * i, piece)
        loads.append(pltpu.make_async_copy(start.at[some], start_in.at[some], sems.at[2 * i]))
        loads.append(pltpu.make_async_copy(field.at[:, some], field_in.at[:, some], sems.at[2 * i + 1]))
    loads.append(pltpu.make_async_copy(end, end_in, sems.at[8]))
    for load in loads:
        load.start()
    tiles = field.shape[2] // LANE
    zero = jnp.zeros((CELLS, LANE), jnp.float32)
    for t in range(tiles, SUB):
        spread = pl.ds(t, CELLS, stride=SUB)
        source[0, spread, :] = zero
        source[1, spread, :] = zero
        curve[spread, :] = zero + (base + 0.9 * slope)
    waves = start_pair()
    march = still()
    for i in range(4):
        loads[2 * i].wait()
        loads[2 * i + 1].wait()
        some = slice(piece * i, piece * (i + 1))
        for t in range(tiles):
            spread, cols = pl.ds(SUB * piece * i + t, piece, stride=SUB), slice(t * LANE, (t + 1) * LANE)
            curve[spread, :] = base + slope * start_in[some, cols]
            source[0, spread, :] = field_in[0, some, cols]
            source[1, spread, :] = field_in[1, some, cols]
        for k in range(piece * i, piece * (i + 1)):
            u, c = (source[0, rows(k), :], source[1, rows(k), :]), curve[rows(k), :]
            march = [march[1], step(c, swing, march[1], march[0], u)]
            waves = [[w[1], step(c, swing, w[1], w[0])] for w in waves]
        if i < 3:
            write_all(snap.at[i], 0, waves[0] + waves[1] + march)
    matrix = waves[0] + waves[1]
    write(own, matrix + list(sums_of(matrix, *march)))
    loads[8].wait()


def stow_kernel(source, curve, end, *packs):
    xbase, xslope, _, _ = constants(CROSS_STIFFNESS)
    tiles = end.shape[1] // LANE
    x = lax.axis_index("xr")
    count = CELLS // 4
    for d, pack in enumerate(packs):
        here = pl.ds(pl.multiple_of((x ^ d) * SUB * count, SUB * count), SUB * count)
        re, im = source[0, here, :], source[1, here, :]
        pack[0] = MIX.real * re - MIX.imag * im
        pack[1] = MIX.real * im + MIX.imag * re
        pack[2] = curve[here, :]
        first = pl.multiple_of((x ^ d) * count, count)
        for t in range(tiles):
            cols = slice(t * LANE, (t + 1) * LANE)
            pack[3, pl.ds(t, count, stride=SUB), :] = xbase + xslope * end[pl.ds(first, count), cols]
        for t in range(tiles, SUB):
            pack[3, pl.ds(t, count, stride=SUB), :] = jnp.zeros((count, LANE), jnp.float32) + (
                xbase + 0.9 * xslope
            )


def turn_kernel(pack, turned):
    turned[...] = pack[3].T


def pair_kernel(axis, bit, own, other, total):
    upper = ((lax.axis_index(axis) >> bit) & 1) == 1
    a, b = read(own), read(other)
    write(total, compose(pick(upper, b, a), pick(upper, a, b)))


def quad_kernel(axis, own, other1, other2, other3, total):
    place = lax.axis_index(axis)
    odd = (place & 1) == 1
    high = (place & 2) == 2
    a, r1, r2, r3 = read(own), read(other1), read(other2), read(other3)
    mine = compose(pick(odd, r1, a), pick(odd, a, r1))
    theirs = compose(pick(odd, r3, r2), pick(odd, r2, r3))
    write(total, compose(pick(high, theirs, mine), pick(high, mine, theirs)))


def descend_pair(left, right, upper, other):
    return (
        pick(upper, normal(advance(left, other)), left),
        pick(upper, right, normal(retreat(right, other))),
    )


def descend_quad(left, right, place, r1, r2, r3):
    odd = (place & 1) == 1
    high = (place & 2) == 2
    first, second = pick(odd, r3, r2), pick(odd, r2, r3)
    left = pick(high, normal(advance(normal(advance(left, first)), second)), left)
    right = pick(high, right, normal(retreat(normal(retreat(right, second)), first)))
    return descend_pair(left, right, odd, r1)


def brace_kernel(own, c1, z1, z2, z3, z4, before, after):
    z, c = lax.axis_index("z"), lax.axis_index("c")
    block, partner = read(own), read(c1)
    second, odd, high, fold = c == 1, (z & 1) == 1, (z & 2) == 2, (z & 4) == 4
    near, far = read(z1), read(z4)
    r2, r3 = read(z2), read(z3)
    pair = compose(pick(odd, r3, r2), pick(odd, r2, r3))
    zero = jnp.zeros((SUB, LANE), jnp.float32)
    one = zero + 1.0
    unit = [(one, zero), (zero, zero), (zero, zero), (one, zero), (zero, zero), (zero, zero)]
    low, up = unit, block
    for flag, other in ((second, partner), (odd, near), (high, pair), (fold, far)):
        low = pick(flag, compose(other, low), low)
        up = pick(flag, up, compose(up, other))
    write_all(before, 0, low)
    write_all(after, 0, up)


def close_kernel(before, after, snap, y1, y2, y3, bound0, bound1, bound2, bound3, bounds):
    x, y = lax.axis_index("xr"), lax.axis_index("y")
    left, right = ends(snap[0, 0])
    left, right = descend_quad(left, right, y, read(y1), read(y2), read(y3))
    left = normal(advance(left, read_all(before, 0, 6)))
    right = normal(retreat(right, read_all(after, 0, 6)))
    v0, v1 = meet(left, right)
    used = lax.broadcasted_iota(jnp.int32, (SUB, LANE), 0) < SPREAD
    for i in range(4):
        a, b = v0, v1
        if i:
            span = read_all(snap.at[i - 1], 0, 6)
            a, b = through(span[:4], v0, v1)
            a, b = add(a, span[4]), add(b, span[5])
        for j, part in enumerate((a, b)):
            bounds[i, 2 * j] = jnp.where(used, MIX.real * part[0] - MIX.imag * part[1], 0.0)
            bounds[i, 2 * j + 1] = jnp.where(used, MIX.real * part[1] + MIX.imag * part[0], 0.0)
    for d, bound in enumerate((bound0, bound1, bound2, bound3)):
        bound[...] = bounds[x ^ d]


LEVELS = ((0, 1), (1, 1), (1, 2), (1, 4), (0, 2), (0, 4))
HALF = CELLS // 2
LATE, WHOLE, SOLVE, OWN, LEVEL0, PER_LEVEL = 8, 16, 24, 32, 36, 16


def upper_of(axis, stride):
    return (lax.broadcasted_iota(jnp.int32, (SUB, LANE), axis) & stride) == stride


def swapped(v, axis, stride, upper):
    size = SUB if axis == 0 else LANE
    down = pltpu.roll(v, stride, axis)
    if 2 * stride == size:
        return down
    return jnp.where(upper, down, pltpu.roll(v, size - stride, axis))


def swapped_all(parts, axis, stride, upper):
    return [(swapped(p[0], axis, stride, upper), swapped(p[1], axis, stride, upper)) for p in parts]


def middle(bound, pack, mid):
    _, _, swing, push = constants(DEPTH_STIFFNESS)
    past, now = (bound[0], bound[1]), (bound[2], bound[3])
    for k in range(CELLS // 4):
        u, c = (pack[0, rows(k), :], pack[1, rows(k), :]), pack[2, rows(k), :]
        mid[0, rows(k), :] = u[0] - push * now[1]
        mid[1, rows(k), :] = u[1] + push * now[0]
        past, now = now, step(c, swing, now, past, u)


def plan_kernel(*refs):
    tiles, bound, pack, (turn0, turn2, pack1, pack3) = refs[0], refs[1], refs[2], refs[3:7]
    curve, plan, first, whole, mid = refs[7:]
    middle(bound, pack, mid)
    first[0] = mid[0].T
    first[1] = mid[1].T
    _, _, swing, _ = constants(CROSS_STIFFNESS)
    x = lax.axis_index("xr")
    whole[x] = turn0[...]
    whole[x ^ 1] = pack1[3].T
    whole[x ^ 2] = turn2[...]
    whole[x ^ 3] = pack3[3].T
    for q in range(4):
        for h in range(2):
            curve[pl.ds(2 * q + h, CELLS, stride=SUB), :] = whole[q, CELLS * h : CELLS * (h + 1), :]
    halves = [start_pair(), start_pair()]
    for k in range(HALF):
        for h in range(2):
            c = curve[rows(k + HALF * h), :]
            halves[h] = [[w[1], step(c, swing, w[1], w[0])] for w in halves[h]]
    early, late = (w[0] + w[1] for w in halves)
    write_all(plan, 0, early)
    write_all(plan, LATE, late)
    matrix = product(late, early)
    write_all(plan, WHOLE, matrix)
    lane = lax.broadcasted_iota(jnp.int32, (SUB, LANE), 1)
    unit = start_pair()
    unit = unit[0] + unit[1]
    matrix = pick((lane & 7) >= tiles, unit, matrix)
    total = matrix
    stages = []
    for i, (axis, stride) in enumerate(LEVELS):
        upper = upper_of(axis, stride)
        other = swapped_all(total, axis, stride, upper)
        low = pick(upper, other, total)
        stages.append((upper, other))
        if i < 5:
            write_all(plan, LEVEL0 + PER_LEVEL * i, low)
            total = product(pick(upper, total, other), low)
    zero = jnp.zeros((SUB, LANE), jnp.float32)
    one = zero + 1.0
    left, right = [(zero, zero), (one, zero)], [(one, zero), (zero, zero)]
    left_weights, right_weights = [], []

    def rescale(pair, weights):
        size = jnp.maximum(
            jnp.maximum(jnp.abs(pair[0][0]), jnp.abs(pair[0][1])),
            jnp.maximum(jnp.abs(pair[1][0]), jnp.abs(pair[1][1])),
        )
        scale = 1.0 / size
        return [scaled(p, scale) for p in pair], [[scaled(w, scale) for w in ws] for ws in weights]

    for upper, other in reversed(stages):
        gone = list(through(other, left[0], left[1]))
        left_weights.append([scaled(p, jnp.where(upper, 1.0, 0.0)) for p in left])
        left, left_weights = rescale(pick(upper, gone, left), left_weights)
        t00, t10, t01, t11 = other
        back = [sub(mul(t11, right[0]), mul(t01, right[1])), sub(mul(t00, right[1]), mul(t10, right[0]))]
        right_weights.append([scaled(p, jnp.where(upper, 0.0, 1.0)) for p in back])
        right, right_weights = rescale(pick(upper, right, back), right_weights)
    t00, t10, t01, t11 = matrix
    right = [sub(mul(t11, right[0]), mul(t01, right[1])), sub(mul(t00, right[1]), mul(t10, right[0]))]
    right_weights.append(right)
    right, right_weights = rescale(right, right_weights)
    det = sub(mul(left[1], right[0]), mul(left[0], right[1]))
    scale = -1.0 / (det[0] * det[0] + det[1] * det[1])
    inverse = (det[0] * scale, -det[1] * scale)
    write_all(plan, SOLVE, [mul(p, inverse) for p in (left[0], right[0], right[1], left[1])])
    write_all(plan, OWN, right_weights[-1])
    for i in range(6):
        write_all(plan, LEVEL0 + PER_LEVEL * i + 8, left_weights[5 - i] + right_weights[5 - i])


def cross_kernel(*refs):
    bounds, packs, curve, plan, first, (result, mid, turned, source, out, sems) = (
        refs[:3], refs[3:6], refs[6], refs[7], refs[8], refs[9:],
    )
    tiles = result.shape[2] // LANE // 4
    x = lax.axis_index("xr")
    lines = CELLS // 4
    turned[x, 0] = first[0]
    turned[x, 1] = first[1]
    for d in range(1, 4):
        middle(bounds[d - 1], packs[d - 1], mid.at[d - 1])
        turned[x ^ d, 0] = mid[d - 1, 0].T
        turned[x ^ d, 1] = mid[d - 1, 1].T
    _, _, swing, push = constants(CROSS_STIFFNESS)
    for q in range(4):
        for h in range(2):
            spread = pl.ds(2 * q + h, CELLS, stride=SUB)
            half = slice(CELLS * h, CELLS * (h + 1))
            source[0, spread, :] = turned[q, 0, half, :]
            source[1, spread, :] = turned[q, 1, half, :]

    def cell(k):
        return (source[0, rows(k), :], source[1, rows(k), :]), curve[rows(k), :]

    marches = [still(), still()]
    for k in range(HALF):
        for h in range(2):
            u, c = cell(k + HALF * h)
            past, now = marches[h]
            marches[h] = [now, step(c, swing, now, past, u)]
    early, late, matrix = (read_all(plan, first, 4) for first in (0, LATE, WHOLE))
    end0, end1 = through(late, *marches[0])
    end0, end1 = add(end0, marches[1][0]), add(end1, marches[1][1])
    valid = (lax.broadcasted_iota(jnp.int32, (SUB, LANE), 1) & 7) < tiles
    zero = jnp.zeros((SUB, LANE), jnp.float32)
    sums = [(jnp.where(valid, s[0], zero), jnp.where(valid, s[1], zero)) for s in sums_of(matrix, end0, end1)]
    w0, w1 = read_all(plan, OWN, 2)
    g, h = (zero, zero), add(mul(w0, sums[0]), mul(w1, sums[1]))
    for i, (axis, stride) in enumerate(LEVELS):
        upper = upper_of(axis, stride)
        other = swapped_all(sums, axis, stride, upper)
        l0, l1, r0, r1 = read_all(plan, LEVEL0 + PER_LEVEL * i + 8, 4)
        g = add(g, add(mul(l0, other[0]), mul(l1, other[1])))
        h = add(h, add(mul(r0, other[0]), mul(r1, other[1])))
        if i < 5:
            t00, t10, t01, t11 = read_all(plan, LEVEL0 + PER_LEVEL * i, 4)
            low, high = pick(upper, other, sums), pick(upper, sums, other)
            sums = [
                add(low[0], add(mul(t00, high[0]), mul(t10, high[1]))),
                add(low[1], add(mul(t01, high[0]), mul(t11, high[1]))),
            ]
    f0, p0, p1, f1 = read_all(plan, SOLVE, 4)
    v0 = add(mul(f0, h), mul(p0, g))
    v1 = add(mul(p1, g), mul(f1, h))
    half = through(early, v0, v1)
    states = [[v0, v1], [add(half[0], marches[0][0]), add(half[1], marches[0][1])]]
    for k in range(HALF):
        for h in range(2):
            u, c = cell(k + HALF * h)
            past, now = states[h]
            source[0, rows(k + HALF * h), :] = u[0] - push * now[1]
            source[1, rows(k + HALF * h), :] = u[1] + push * now[0]
            states[h] = [now, step(c, swing, now, past, u)]
    stores = []
    for q in range(4):
        for part in range(2):
            halves = [source[part, pl.ds(2 * q + h, CELLS, stride=SUB), :] for h in range(2)]
            turned[q, part] = jnp.concatenate(halves, axis=0).T
            for t in range(tiles):
                cols = slice((q * tiles + t) * LANE, (q * tiles + t + 1) * LANE)
                out[part, :, cols] = turned[q, part, pl.ds(t, lines, stride=SUB), :]
        whole = pl.ds(q * tiles * LANE, tiles * LANE)
        store = pltpu.make_async_copy(out.at[:, :, whole], result.at[:, :, whole], sems.at[q])
        store.start()
        stores.append(store)
    for store in stores:
        store.wait()


def shaped(*shape):
    return jax.ShapeDtypeStruct(shape, jnp.float32)


def call(kernel, outs, scratch=(), far_in=False, far_out=False):
    far, here = pl.BlockSpec(memory_space=pltpu.HBM), pl.BlockSpec(memory_space=pltpu.VMEM)
    out_specs = [far if far_out else here] * len(outs) if isinstance(outs, list) else (far if far_out else here)

    def run(*values):
        return pl.pallas_call(
            kernel,
            out_shape=outs,
            in_specs=[far if far_in else here] * len(values),
            out_specs=out_specs,
            scratch_shapes=list(scratch),
            compiler_params=pltpu.CompilerParams(vmem_limit_bytes=8 << 20),
            cost_estimate=pl.CostEstimate(flops=100000, bytes_accessed=1000000, transcendentals=0),
        )(*values)

    return run


def local(sound_field, index_start, index_end):
    span_shape = shaped(9 * SUB, LANE)
    cells = SUB * CELLS
    piece = cells // 4
    inputs = (sound_field, index_start, index_end)
    own, snap, source, curve, end = call(
        open_kernel,
        [
            span_shape,
            shaped(3, PARTS, SUB, LANE),
            shaped(2, cells, LANE),
            shaped(cells, LANE),
            shaped(*index_end.shape),
        ],
        [pltpu.VMEM(v.shape, jnp.float32) for v in inputs[:2]] + [pltpu.SemaphoreType.DMA((9,))],
        far_in=True,
    )(*(pltpu.with_memory_space_constraint(v, pltpu.HBM) for v in inputs))
    packs = call(stow_kernel, [shaped(4, piece, LANE)] * 4)(source, curve, end)

    def flip(value, axis, d):
        return lax.ppermute(value, axis, [(i, i ^ d) for i in range(lax.axis_size(axis))])

    def pair(axis, bit, a, b):
        return call(lambda *refs: pair_kernel(axis, bit, *refs), span_shape)(a, b)

    def quad(axis, a, others):
        return call(lambda *refs: quad_kernel(axis, *refs), span_shape)(a, *others)

    c1 = flip(own, "c", 1)
    total = pair("c", 0, own, c1)
    zs = [flip(total, "z", d) for d in (1, 2, 3)]
    total = quad("z", total, zs)
    z4 = lax.ppermute(total, "z", [(i, 7 - i) for i in range(8)])
    total = pair("z", 2, total, z4)
    ys = [flip(total, "y", d) for d in (1, 2, 3)]
    before, after = call(brace_kernel, [shaped(PARTS, SUB, LANE)] * 2)(own, c1, *zs, z4)
    bounds = call(
        close_kernel, [shaped(4, SUB, LANE)] * 4, [pltpu.VMEM((4, 4, SUB, LANE), jnp.float32)]
    )(before, after, snap, *ys)
    packs = [packs[0]] + [flip(packs[d], "xr", d) for d in (1, 2, 3)]
    turns = []
    for d in TURNS:
        turns.append(call(turn_kernel, shaped(LANE, LANE))(packs[d]))
    bounds = [bounds[0]] + [flip(bounds[d], "xr", d) for d in (1, 2, 3)]
    tiles = sound_field.shape[2] // LANE
    curve, plan, first = call(
        lambda *refs: plan_kernel(tiles, *refs),
        [shaped(cells, LANE), shaped(LEVEL0 + 6 * PER_LEVEL, SUB, LANE), shaped(2, LANE, LANE)],
        [pltpu.VMEM((4, LANE, LANE), jnp.float32), pltpu.VMEM((2, piece, LANE), jnp.float32)],
    )(bounds[0], packs[0], *turns, packs[1], packs[3])
    result = shaped(2, CELLS // 4, 4 * sound_field.shape[2])
    return call(
        cross_kernel,
        result,
        [
            pltpu.VMEM((3, 2, piece, LANE), jnp.float32),
            pltpu.VMEM((4, 2, LANE, LANE), jnp.float32),
            pltpu.VMEM((2, cells, LANE), jnp.float32),
            pltpu.VMEM(result.shape, jnp.float32),
            pltpu.SemaphoreType.DMA((4,)),
        ],
        far_out=True,
    )(*bounds[1:], *packs[1:], curve, plan, first)


TURNS = (0, 2)


def solution(mesh):
    split = Mesh(mesh.devices.reshape(4, 8, 2, mesh.shape["xr"]), DEPTH + ("xr",))
    in_specs = (P(None, DEPTH, "xr"), P(DEPTH, "xr"), P(DEPTH, "xr"))
    out_specs = P(None, DEPTH + ("xr",), None)

    return jax.shard_map(local, mesh=split, in_specs=in_specs, out_specs=out_specs, check_vma=False)
```

profile of v0, /device:TPU:24, one launch (start us, length us, event | category | flops | bytes accessed | tf_op | source)
XLA Modules:
  0.0 45.5 jit_solution(4144867832376032050)
XLA Ops:
  0.0 1.4 %shard_map.37 = (f32[72,128]{1,0:T(8,128)S(1)}, f32[3,12,8,128]{3,2,1,0:T(8,128)S(1)}, f32[2,512,128]{2,1,0:T(8,128)S(1)}, f32[512,128]{1,0:T(8,128)S(1)}, f32[64,896]{1,0:T(8,128)S(1)}) custom-call(f32[2,64,896]{2,1,0:T(8,128)} %field.1, f32[64,896]{1,0:T(8,128)} %start.1, f32[64,896]{1,0:T(8,128)} %end.1), custom_call_target="tpu_custom_call" | custom-call | flops 100000 | bytes 1000000 | tf_op jit(solution)/shard_map/pallas_call | solution.py:507
  1.4 0.1 shard_map.43
  1.6 3.1 %collective-permute-start.12 = (f32[4,128,128]{2,1,0:T(8,128)S(1)}, f32[4,128,128]{2,1,0:T(8,128)S(1)}, u32[]{:S(2)}, u32[]{:S(2)}) collective-permute-start(f32[4,128,128]{2,1,0:T(8,128)S(1)} %get-tuple-element.34), channel_id=1, source_target_pairs={{0,2},{1,3},{2,0},{3,1},{4,6},{5,7},{6,4},{7,5},{8,10},{9,11},{10,... | collective-permute-start | bytes 786440 | tf_op jit(solution)/shard_map/ppermute | solution.py:540
  4.7 0.6 %collective-permute-start.11 = (f32[4,128,128]{2,1,0:T(8,128)S(1)}, f32[4,128,128]{2,1,0:T(8,128)S(1)}, u32[]{:S(2)}, u32[]{:S(2)}) collective-permute-start(f32[4,128,128]{2,1,0:T(8,128)S(1)} %get-tuple-element.33), channel_id=1, source_target_pairs={{0,1},{1,0},{2,3},{3,2},{4,5},{5,4},{6,7},{7,6},{8,9},{9,8},{10,11... | collective-permute-start | bytes 786440 | tf_op jit(solution)/shard_map/ppermute | solution.py:540
  5.3 0.6 %collective-permute-start.13 = (f32[4,128,128]{2,1,0:T(8,128)S(1)}, f32[4,128,128]{2,1,0:T(8,128)S(1)}, u32[]{:S(2)}, u32[]{:S(2)}) collective-permute-start(f32[4,128,128]{2,1,0:T(8,128)S(1)} %get-tuple-element.35), channel_id=1, source_target_pairs={{0,3},{1,2},{2,1},{3,0},{4,7},{5,6},{6,5},{7,4},{8,11},{9,10},{10,... | collective-permute-start | bytes 786440 | tf_op jit(solution)/shard_map/ppermute | solution.py:540
  5.9 0.0 collective-permute-start
  5.9 1.2 %collective-permute-done.refs_1_.c1 = f32[72,128]{1,0:T(8,128)S(1)} collective-permute-done((f32[72,128]{1,0:T(8,128)S(1)}, f32[72,128]{1,0:T(8,128)S(1)}, u32[]{:S(2)}, u32[]{:S(2)}) %collective-permute-start) | collective-permute-done | bytes 36896 | tf_op jit(solution)/shard_map/ppermute | solution.py:540
  7.1 4.7 %collective-permute-start.3 = (f32[72,128]{1,0:T(8,128)S(1)}, f32[72,128]{1,0:T(8,128)S(1)}, u32[]{:S(2)}, u32[]{:S(2)}) collective-permute-start(f32[72,128]{1,0:T(8,128)S(1)} %shard_map.38.refs_0_), channel_id=1, source_target_pairs={{0,24},{8,16},{16,8},{24,0},{32,56},{40,48},{48,40},{56,32},{1,25}... | collective-permute-start | bytes 110600 | tf_op jit(solution)/shard_map/ppermute | solution.py:540
  11.8 1.9 %collective-permute-done.3.refs_3_.z3 = f32[72,128]{1,0:T(8,128)S(1)} collective-permute-done((f32[72,128]{1,0:T(8,128)S(1)}, f32[72,128]{1,0:T(8,128)S(1)}, u32[]{:S(2)}, u32[]{:S(2)}) %collective-permute-start.3) | collective-permute-done | bytes 36896 | tf_op jit(solution)/shard_map/ppermute | solution.py:540
  13.8 2.9 %collective-permute-done.2.refs_2_.z2 = f32[72,128]{1,0:T(8,128)S(1)} collective-permute-done((f32[72,128]{1,0:T(8,128)S(1)}, f32[72,128]{1,0:T(8,128)S(1)}, u32[]{:S(2)}, u32[]{:S(2)}) %collective-permute-start.2) | collective-permute-done | bytes 36896 | tf_op jit(solution)/shard_map/ppermute | solution.py:540
  16.7 1.0 %collective-permute-done.1.refs_1_.z1 = f32[72,128]{1,0:T(8,128)S(1)} collective-permute-done((f32[72,128]{1,0:T(8,128)S(1)}, f32[72,128]{1,0:T(8,128)S(1)}, u32[]{:S(2)}, u32[]{:S(2)}) %collective-permute-start.1) | collective-permute-done | bytes 36896 | tf_op jit(solution)/shard_map/ppermute | solution.py:540
  17.7 0.1 shard_map.39.refs_0_
  17.8 5.5 %collective-permute-start.4 = (f32[72,128]{1,0:T(8,128)S(1)}, f32[72,128]{1,0:T(8,128)S(1)}, u32[]{:S(2)}, u32[]{:S(2)}) collective-permute-start(f32[72,128]{1,0:T(8,128)S(1)} %shard_map.39.refs_0_), channel_id=1, source_target_pairs={{0,56},{8,48},{16,40},{24,32},{32,24},{40,16},{48,8},{56,0},{1,57}... | collective-permute-start | bytes 110600 | tf_op jit(solution)/shard_map/ppermute | solution.py:552
  23.3 1.9 %collective-permute-done.4.z4.refs_1_ = f32[72,128]{1,0:T(8,128)S(1)} collective-permute-done((f32[72,128]{1,0:T(8,128)S(1)}, f32[72,128]{1,0:T(8,128)S(1)}, u32[]{:S(2)}, u32[]{:S(2)}) %collective-permute-start.4) | collective-permute-done | bytes 36896 | tf_op jit(solution)/shard_map/ppermute | solution.py:552
  25.2 0.3 collective-permute-start.7
  25.5 2.6 %collective-permute-start.6 = (f32[72,128]{1,0:T(8,128)S(1)}, f32[72,128]{1,0:T(8,128)S(1)}, u32[]{:S(2)}, u32[]{:S(2)}) collective-permute-start(f32[72,128]{1,0:T(8,128)S(1)} %shard_map.41), channel_id=1, source_target_pairs={{0,128},{64,192},{128,0},{192,64},{1,129},{65,193},{129,1},{193,65... | collective-permute-start | bytes 110600 | tf_op jit(solution)/shard_map/ppermute | solution.py:540
  28.1 2.4 %collective-permute-done.7.y3 = f32[72,128]{1,0:T(8,128)S(1)} collective-permute-done((f32[72,128]{1,0:T(8,128)S(1)}, f32[72,128]{1,0:T(8,128)S(1)}, u32[]{:S(2)}, u32[]{:S(2)}) %collective-permute-start.7) | collective-permute-done | bytes 36896 | tf_op jit(solution)/shard_map/ppermute | solution.py:540
  30.5 0.0 collective-permute-start.5
  30.5 0.2 shard_map.40
  30.7 0.4 collective-permute-done.6.y2
  31.0 3.4 %collective-permute-done.5.y1 = f32[72,128]{1,0:T(8,128)S(1)} collective-permute-done((f32[72,128]{1,0:T(8,128)S(1)}, f32[72,128]{1,0:T(8,128)S(1)}, u32[]{:S(2)}, u32[]{:S(2)}) %collective-permute-start.5) | collective-permute-done | bytes 36896 | tf_op jit(solution)/shard_map/ppermute | solution.py:540
  34.5 0.1 shard_map.42
  34.6 1.4 %collective-permute-start.8 = (f32[4,8,128]{2,1,0:T(8,128)S(1)}, f32[4,8,128]{2,1,0:T(8,128)S(1)}, u32[]{:S(2)}, u32[]{:S(2)}) collective-permute-start(f32[4,8,128]{2,1,0:T(8,128)S(1)} %get-tuple-element.27), channel_id=1, source_target_pairs={{0,1},{1,0},{2,3},{3,2},{4,5},{5,4},{6,7},{7,6},{8,9},{9,8},{10,11... | collective-permute-start | bytes 49160 | tf_op jit(solution)/shard_map/ppermute | solution.py:540
  36.0 2.8 %collective-permute-start.9 = (f32[4,8,128]{2,1,0:T(8,128)S(1)}, f32[4,8,128]{2,1,0:T(8,128)S(1)}, u32[]{:S(2)}, u32[]{:S(2)}) collective-permute-start(f32[4,8,128]{2,1,0:T(8,128)S(1)} %get-tuple-element.28), channel_id=1, source_target_pairs={{0,2},{1,3},{2,0},{3,1},{4,6},{5,7},{6,4},{7,5},{8,10},{9,11},{10,... | collective-permute-start | bytes 49160 | tf_op jit(solution)/shard_map/ppermute | solution.py:540
  38.8 0.0 collective-permute-done.12.pack.refs_4_
  38.8 0.6 %collective-permute-start.10 = (f32[4,8,128]{2,1,0:T(8,128)S(1)}, f32[4,8,128]{2,1,0:T(8,128)S(1)}, u32[]{:S(2)}, u32[]{:S(2)}) collective-permute-start(f32[4,8,128]{2,1,0:T(8,128)S(1)} %get-tuple-element.29), channel_id=1, source_target_pairs={{0,3},{1,2},{2,1},{3,0},{4,7},{5,6},{6,5},{7,4},{8,11},{9,10},{10,... | collective-permute-start | bytes 49160 | tf_op jit(solution)/shard_map/ppermute | solution.py:540
  39.4 0.1 shard_map.44.refs_2_
  39.5 0.1 shard_map.45.refs_3_
  39.6 0.7 %shard_map.46 = (f32[512,128]{1,0:T(8,128)S(1)}, f32[132,8,128]{2,1,0:T(8,128)S(1)}, f32[2,128,128]{2,1,0:T(8,128)S(1)}) custom-call(f32[4,8,128]{2,1,0:T(8,128)S(1)} %get-tuple-element.36.refs_0_, f32[4,128,128]{2,1,0:T(8,128)S(1)} %get-tuple-element.37.pack.refs_1_, f32[128,128]{1,0:T(8,128)S(1)} %shard_map.44.refs_2_, f32[128,128]{1,0:T(8,128)S(1)} %shard_map.45.refs_3_, ...), custom_call_target="tpu_custom_call" | custom-call | flops 100000 | bytes 1000000 | tf_op jit(solution)/shard_map/pallas_call | solution.py:507
  40.3 0.9 %collective-permute-done.9.refs_1_ = f32[4,8,128]{2,1,0:T(8,128)S(1)} collective-permute-done((f32[4,8,128]{2,1,0:T(8,128)S(1)}, f32[4,8,128]{2,1,0:T(8,128)S(1)}, u32[]{:S(2)}, u32[]{:S(2)}) %collective-permute-start.9) | collective-permute-done | bytes 16416 | tf_op jit(solution)/shard_map/ppermute | solution.py:540
  41.3 2.5 %collective-permute-done.10.refs_2_ = f32[4,8,128]{2,1,0:T(8,128)S(1)} collective-permute-done((f32[4,8,128]{2,1,0:T(8,128)S(1)}, f32[4,8,128]{2,1,0:T(8,128)S(1)}, u32[]{:S(2)}, u32[]{:S(2)}) %collective-permute-start.10) | collective-permute-done | bytes 16416 | tf_op jit(solution)/shard_map/ppermute | solution.py:540
  43.8 1.8 %shard_map.47 = f32[2,16,3584]{2,1,0:T(8,128)} custom-call(f32[4,8,128]{2,1,0:T(8,128)S(1)} %collective-permute-done.8.refs_0_, f32[4,8,128]{2,1,0:T(8,128)S(1)} %collective-permute-done.9.refs_1_, f32[4,8,128]{2,1,0:T(8,128)S(1)} %collective-permute-done.10.refs_2_, f32[4,128,128]{2,1,0:T(8,128)S(1)} %collective-permute-done.11.refs_4_.refs_3_, ...), custom_call_target="tpu_custom_call" | custom-call | flops 100000 | bytes 1000000 | tf_op jit(solution)/shard_map/pallas_call | solution.py:507
  (7 shorter events, 0.1 us)
Async XLA Ops:
  1.6 37.2 %collective-permute-start.12 = (f32[4,128,128]{2,1,0:T(8,128)S(1)}, f32[4,128,128]{2,1,0:T(8,128)S(1)}, u32[]{:S(2)}, u32[]{:S(2)}) collective-permute-start(f32[4,128,128]{2,1,0:T(8,128)S(1)} %get-tuple-element.34), channel_id=1, source_target_pairs={{0,2},{1,3},{2,0},{3,1},{4,6},{5,7},{6,4},{7,5},{8,10},{9,11},{10,... | collective-permute-start | bytes 786440 | tf_op jit(solution)/shard_map/ppermute | solution.py:540
  4.7 34.9 %collective-permute-start.11 = (f32[4,128,128]{2,1,0:T(8,128)S(1)}, f32[4,128,128]{2,1,0:T(8,128)S(1)}, u32[]{:S(2)}, u32[]{:S(2)}) collective-permute-start(f32[4,128,128]{2,1,0:T(8,128)S(1)} %get-tuple-element.33), channel_id=1, source_target_pairs={{0,1},{1,0},{2,3},{3,2},{4,5},{5,4},{6,7},{7,6},{8,9},{9,8},{10,11... | collective-permute-start | bytes 786440 | tf_op jit(solution)/shard_map/ppermute | solution.py:540
  5.3 34.3 %collective-permute-start.13 = (f32[4,128,128]{2,1,0:T(8,128)S(1)}, f32[4,128,128]{2,1,0:T(8,128)S(1)}, u32[]{:S(2)}, u32[]{:S(2)}) collective-permute-start(f32[4,128,128]{2,1,0:T(8,128)S(1)} %get-tuple-element.35), channel_id=1, source_target_pairs={{0,3},{1,2},{2,1},{3,0},{4,7},{5,6},{6,5},{7,4},{8,11},{9,10},{10,... | collective-permute-start | bytes 786440 | tf_op jit(solution)/shard_map/ppermute | solution.py:540
  5.9 1.2 %collective-permute-start = (f32[72,128]{1,0:T(8,128)S(1)}, f32[72,128]{1,0:T(8,128)S(1)}, u32[]{:S(2)}, u32[]{:S(2)}) collective-permute-start(f32[72,128]{1,0:T(8,128)S(1)} %get-tuple-element.23.refs_0_.own), channel_id=1, source_target_pairs={{0,4},{4,0},{1,5},{5,1},{2,6},{6,2},{3,7},{7,3},{8,12},{12,8},{9,1... | collective-permute-start | bytes 110600 | tf_op jit(solution)/shard_map/ppermute | solution.py:540
  7.1 6.6 %collective-permute-start.3 = (f32[72,128]{1,0:T(8,128)S(1)}, f32[72,128]{1,0:T(8,128)S(1)}, u32[]{:S(2)}, u32[]{:S(2)}) collective-permute-start(f32[72,128]{1,0:T(8,128)S(1)} %shard_map.38.refs_0_), channel_id=1, source_target_pairs={{0,24},{8,16},{16,8},{24,0},{32,56},{40,48},{48,40},{56,32},{1,25}... | collective-permute-start | bytes 110600 | tf_op jit(solution)/shard_map/ppermute | solution.py:540
  11.8 4.9 %collective-permute-start.2 = (f32[72,128]{1,0:T(8,128)S(1)}, f32[72,128]{1,0:T(8,128)S(1)}, u32[]{:S(2)}, u32[]{:S(2)}) collective-permute-start(f32[72,128]{1,0:T(8,128)S(1)} %shard_map.38.refs_0_), channel_id=1, source_target_pairs={{0,16},{8,24},{16,0},{24,8},{32,48},{40,56},{48,32},{56,40},{1,17}... | collective-permute-start | bytes 110600 | tf_op jit(solution)/shard_map/ppermute | solution.py:540
  13.8 4.0 %collective-permute-start.1 = (f32[72,128]{1,0:T(8,128)S(1)}, f32[72,128]{1,0:T(8,128)S(1)}, u32[]{:S(2)}, u32[]{:S(2)}) collective-permute-start(f32[72,128]{1,0:T(8,128)S(1)} %shard_map.38.refs_0_), channel_id=1, source_target_pairs={{0,8},{8,0},{16,24},{24,16},{32,40},{40,32},{48,56},{56,48},{1,9},... | collective-permute-start | bytes 110600 | tf_op jit(solution)/shard_map/ppermute | solution.py:540
  17.8 7.4 %collective-permute-start.4 = (f32[72,128]{1,0:T(8,128)S(1)}, f32[72,128]{1,0:T(8,128)S(1)}, u32[]{:S(2)}, u32[]{:S(2)}) collective-permute-start(f32[72,128]{1,0:T(8,128)S(1)} %shard_map.39.refs_0_), channel_id=1, source_target_pairs={{0,56},{8,48},{16,40},{24,32},{32,24},{40,16},{48,8},{56,0},{1,57}... | collective-permute-start | bytes 110600 | tf_op jit(solution)/shard_map/ppermute | solution.py:552
  25.2 5.3 %collective-permute-start.7 = (f32[72,128]{1,0:T(8,128)S(1)}, f32[72,128]{1,0:T(8,128)S(1)}, u32[]{:S(2)}, u32[]{:S(2)}) collective-permute-start(f32[72,128]{1,0:T(8,128)S(1)} %shard_map.41), channel_id=1, source_target_pairs={{0,192},{64,128},{128,64},{192,0},{1,193},{65,129},{129,65},{193,1... | collective-permute-start | bytes 110600 | tf_op jit(solution)/shard_map/ppermute | solution.py:540
  25.5 5.5 %collective-permute-start.6 = (f32[72,128]{1,0:T(8,128)S(1)}, f32[72,128]{1,0:T(8,128)S(1)}, u32[]{:S(2)}, u32[]{:S(2)}) collective-permute-start(f32[72,128]{1,0:T(8,128)S(1)} %shard_map.41), channel_id=1, source_target_pairs={{0,128},{64,192},{128,0},{192,64},{1,129},{65,193},{129,1},{193,65... | collective-permute-start | bytes 110600 | tf_op jit(solution)/shard_map/ppermute | solution.py:540
  30.5 4.0 %collective-permute-start.5 = (f32[72,128]{1,0:T(8,128)S(1)}, f32[72,128]{1,0:T(8,128)S(1)}, u32[]{:S(2)}, u32[]{:S(2)}) collective-permute-start(f32[72,128]{1,0:T(8,128)S(1)} %shard_map.41), channel_id=1, source_target_pairs={{0,64},{64,0},{128,192},{192,128},{1,65},{65,1},{129,193},{193,129... | collective-permute-start | bytes 110600 | tf_op jit(solution)/shard_map/ppermute | solution.py:540
  34.6 5.7 %collective-permute-start.8 = (f32[4,8,128]{2,1,0:T(8,128)S(1)}, f32[4,8,128]{2,1,0:T(8,128)S(1)}, u32[]{:S(2)}, u32[]{:S(2)}) collective-permute-start(f32[4,8,128]{2,1,0:T(8,128)S(1)} %get-tuple-element.27), channel_id=1, source_target_pairs={{0,1},{1,0},{2,3},{3,2},{4,5},{5,4},{6,7},{7,6},{8,9},{9,8},{10,11... | collective-permute-start | bytes 49160 | tf_op jit(solution)/shard_map/ppermute | solution.py:540
  36.0 5.2 %collective-permute-start.9 = (f32[4,8,128]{2,1,0:T(8,128)S(1)}, f32[4,8,128]{2,1,0:T(8,128)S(1)}, u32[]{:S(2)}, u32[]{:S(2)}) collective-permute-start(f32[4,8,128]{2,1,0:T(8,128)S(1)} %get-tuple-element.28), channel_id=1, source_target_pairs={{0,2},{1,3},{2,0},{3,1},{4,6},{5,7},{6,4},{7,5},{8,10},{9,11},{10,... | collective-permute-start | bytes 49160 | tf_op jit(solution)/shard_map/ppermute | solution.py:540
  38.8 5.0 %collective-permute-start.10 = (f32[4,8,128]{2,1,0:T(8,128)S(1)}, f32[4,8,128]{2,1,0:T(8,128)S(1)}, u32[]{:S(2)}, u32[]{:S(2)}) collective-permute-start(f32[4,8,128]{2,1,0:T(8,128)S(1)} %get-tuple-element.29), channel_id=1, source_target_pairs={{0,3},{1,2},{2,1},{3,0},{4,7},{5,6},{6,5},{7,4},{8,11},{9,10},{10,... | collective-permute-start | bytes 49160 | tf_op jit(solution)/shard_map/ppermute | solution.py:540
where the time goes:
time: 45.6 us; the launch traced here: 45.5 us
  starting transfers between devices  22.1 us (48%)
  waiting for transfers between devices  18.6 us (41%)
  Pallas kernels  4.68 us (10%)
    ppermute x13, waiting for transfers between devices, flip(): lax.ppermute(value, axis, [(i, i ^ d) for i in range(lax.axis_size(axis))])  16.7 us
    ppermute x13, starting transfers between devices, flip(): lax.ppermute(value, axis, [(i, i ^ d) for i in range(lax.axis_size(axis))])  16.7 us
    ppermute x1, starting transfers between devices, local(): z4 = lax.ppermute(total, 'z', [(i, 7 - i) for i in range(8)])  5.47 us
    pallas_call x11, Pallas kernels, run(): pl.pallas_call(kernel, out_shape=outs, in_specs=[far if far_in else here]...  4.68 us
    ppermute x1, waiting for transfers between devices, local(): z4 = lax.ppermute(total, 'z', [(i, 7 - i) for i in range(8)])  1.94 us
  transfers between devices with their start and end apart: 14, of which 10 were waited for; matrix products, arithmetic and copies ran while one was open for 0% of the time, Pallas kernels for 3%

commit v1 on v0

--- a/solution.py
+++ b/solution.py
@@ -344,17 +344,15 @@
 
 
 def plan_kernel(*refs):
-    tiles, bound, pack, (turn0, turn2, pack1, pack3) = refs[0], refs[1], refs[2], refs[3:7]
+    tiles, bound, pack, turns, last = refs[0], refs[1], refs[2], refs[3:6], refs[6]
     curve, plan, first, whole, mid = refs[7:]
     middle(bound, pack, mid)
     first[0] = mid[0].T
     first[1] = mid[1].T
     _, _, swing, _ = constants(CROSS_STIFFNESS)
     x = lax.axis_index("xr")
-    whole[x] = turn0[...]
-    whole[x ^ 1] = pack1[3].T
-    whole[x ^ 2] = turn2[...]
-    whole[x ^ 3] = pack3[3].T
+    for d in range(4):
+        whole[x ^ d] = turns[d][...] if d < 3 else last[3].T
     for q in range(4):
         for h in range(2):
             curve[pl.ds(2 * q + h, CELLS, stride=SUB), :] = whole[q, CELLS * h : CELLS * (h + 1), :]
@@ -487,10 +485,12 @@
             for t in range(tiles):
                 cols = slice((q * tiles + t) * LANE, (q * tiles + t + 1) * LANE)
                 out[part, :, cols] = turned[q, part, pl.ds(t, lines, stride=SUB), :]
-        whole = pl.ds(q * tiles * LANE, tiles * LANE)
-        store = pltpu.make_async_copy(out.at[:, :, whole], result.at[:, :, whole], sems.at[q])
-        store.start()
-        stores.append(store)
+            whole = pl.ds(q * tiles * LANE, tiles * LANE)
+            store = pltpu.make_async_copy(
+                out.at[part, :, whole], result.at[part, :, whole], sems.at[4 * part + q]
+            )
+            store.start()
+            stores.append(store)
     for store in stores:
         store.wait()
 
@@ -566,7 +566,7 @@
         lambda *refs: plan_kernel(tiles, *refs),
         [shaped(cells, LANE), shaped(LEVEL0 + 6 * PER_LEVEL, SUB, LANE), shaped(2, LANE, LANE)],
         [pltpu.VMEM((4, LANE, LANE), jnp.float32), pltpu.VMEM((2, piece, LANE), jnp.float32)],
-    )(bounds[0], packs[0], *turns, packs[1], packs[3])
+    )(bounds[0], packs[0], *turns, packs[3])
     result = shaped(2, CELLS // 4, 4 * sound_field.shape[2])
     return call(
         cross_kernel,
@@ -576,13 +576,13 @@
             pltpu.VMEM((4, 2, LANE, LANE), jnp.float32),
             pltpu.VMEM((2, cells, LANE), jnp.float32),
             pltpu.VMEM(result.shape, jnp.float32),
-            pltpu.SemaphoreType.DMA((4,)),
+            pltpu.SemaphoreType.DMA((8,)),
         ],
         far_out=True,
     )(*bounds[1:], *packs[1:], curve, plan, first)
 
 
-TURNS = (0, 2)
+TURNS = (0, 1, 2)
 
 
 def solution(mesh):

time: 45.6 us -> 46.3 us (1.015)
  starting transfers between devices: 22.1 us -> 22.6 us
    ppermute x13, starting transfers between devices: 16.7 us -> 17.2 us  [flip(): lax.ppermute(value, axis, [(i, i ^ d) for i in range(lax.axis_size(axis))])]
    pallas_call x11 -> x12, Pallas kernels: 4.68 us -> 4.8 us  [run(): pl.pallas_call(kernel, out_shape=outs, in_specs=[far if far_in else here]...]
where the time goes in v1:
time: 46.3 us; the launch traced here: 46.2 us
  starting transfers between devices  22.6 us (49%)
  waiting for transfers between devices  18.7 us (40%)
  Pallas kernels  4.8 us (10%)
    ppermute x13, starting transfers between devices, flip(): lax.ppermute(value, axis, [(i, i ^ d) for i in range(lax.axis_size(axis))])  17.2 us
    ppermute x13, waiting for transfers between devices, flip(): lax.ppermute(value, axis, [(i, i ^ d) for i in range(lax.axis_size(axis))])  16.8 us
    ppermute x1, starting transfers between devices, local(): z4 = lax.ppermute(total, 'z', [(i, 7 - i) for i in range(8)])  5.38 us
    pallas_call x12, Pallas kernels, run(): pl.pallas_call(kernel, out_shape=outs, in_specs=[far if far_in else here]...  4.8 us
    ppermute x1, waiting for transfers between devices, local(): z4 = lax.ppermute(total, 'z', [(i, 7 - i) for i in range(8)])  1.94 us
  transfers between devices with their start and end apart: 14, of which 10 were waited for; matrix products, arithmetic and copies ran while one was open for 0% of the time, Pallas kernels for 3%

profile of v1, /device:TPU:24, one launch (start us, length us, event | category | flops | bytes accessed | tf_op | source)
XLA Modules:
  0.0 46.2 jit_solution(8740802679664213163)
XLA Ops:
  0.0 1.4 %shard_map.37 = (f32[72,128]{1,0:T(8,128)S(1)}, f32[3,12,8,128]{3,2,1,0:T(8,128)S(1)}, f32[2,512,128]{2,1,0:T(8,128)S(1)}, f32[512,128]{1,0:T(8,128)S(1)}, f32[64,896]{1,0:T(8,128)S(1)}) custom-call(f32[2,64,896]{2,1,0:T(8,128)} %field.1, f32[64,896]{1,0:T(8,128)} %start.1, f32[64,896]{1,0:T(8,128)} %end.1), custom_call_target="tpu_custom_call" | custom-call | flops 100000 | bytes 1000000 | tf_op jit(solution)/shard_map/pallas_call | solution.py:507
  1.4 0.1 shard_map.43
  1.6 1.6 %collective-permute-start.11 = (f32[4,128,128]{2,1,0:T(8,128)S(1)}, f32[4,128,128]{2,1,0:T(8,128)S(1)}, u32[]{:S(2)}, u32[]{:S(2)}) collective-permute-start(f32[4,128,128]{2,1,0:T(8,128)S(1)} %get-tuple-element.33), channel_id=1, source_target_pairs={{0,1},{1,0},{2,3},{3,2},{4,5},{5,4},{6,7},{7,6},{8,9},{9,8},{10,11... | collective-permute-start | bytes 786440 | tf_op jit(solution)/shard_map/ppermute | solution.py:540
  3.2 2.7 %collective-permute-start.12 = (f32[4,128,128]{2,1,0:T(8,128)S(1)}, f32[4,128,128]{2,1,0:T(8,128)S(1)}, u32[]{:S(2)}, u32[]{:S(2)}) collective-permute-start(f32[4,128,128]{2,1,0:T(8,128)S(1)} %get-tuple-element.34), channel_id=1, source_target_pairs={{0,2},{1,3},{2,0},{3,1},{4,6},{5,7},{6,4},{7,5},{8,10},{9,11},{10,... | collective-permute-start | bytes 786440 | tf_op jit(solution)/shard_map/ppermute | solution.py:540
  5.9 0.5 %collective-permute-start.13 = (f32[4,128,128]{2,1,0:T(8,128)S(1)}, f32[4,128,128]{2,1,0:T(8,128)S(1)}, u32[]{:S(2)}, u32[]{:S(2)}) collective-permute-start(f32[4,128,128]{2,1,0:T(8,128)S(1)} %get-tuple-element.35), channel_id=1, source_target_pairs={{0,3},{1,2},{2,1},{3,0},{4,7},{5,6},{6,5},{7,4},{8,11},{9,10},{10,... | collective-permute-start | bytes 786440 | tf_op jit(solution)/shard_map/ppermute | solution.py:540
  6.4 1.2 %collective-permute-done.refs_1_.c1 = f32[72,128]{1,0:T(8,128)S(1)} collective-permute-done((f32[72,128]{1,0:T(8,128)S(1)}, f32[72,128]{1,0:T(8,128)S(1)}, u32[]{:S(2)}, u32[]{:S(2)}) %collective-permute-start) | collective-permute-done | bytes 36896 | tf_op jit(solution)/shard_map/ppermute | solution.py:540
  7.6 4.7 %collective-permute-start.3 = (f32[72,128]{1,0:T(8,128)S(1)}, f32[72,128]{1,0:T(8,128)S(1)}, u32[]{:S(2)}, u32[]{:S(2)}) collective-permute-start(f32[72,128]{1,0:T(8,128)S(1)} %shard_map.38.refs_0_), channel_id=1, source_target_pairs={{0,24},{8,16},{16,8},{24,0},{32,56},{40,48},{48,40},{56,32},{1,25}... | collective-permute-start | bytes 110600 | tf_op jit(solution)/shard_map/ppermute | solution.py:540
  12.4 0.0 collective-permute-start.2
  12.4 1.9 %collective-permute-done.3.refs_3_.z3 = f32[72,128]{1,0:T(8,128)S(1)} collective-permute-done((f32[72,128]{1,0:T(8,128)S(1)}, f32[72,128]{1,0:T(8,128)S(1)}, u32[]{:S(2)}, u32[]{:S(2)}) %collective-permute-start.3) | collective-permute-done | bytes 36896 | tf_op jit(solution)/shard_map/ppermute | solution.py:540
  14.3 0.0 collective-permute-start.1
  14.3 3.0 %collective-permute-done.2.refs_2_.z2 = f32[72,128]{1,0:T(8,128)S(1)} collective-permute-done((f32[72,128]{1,0:T(8,128)S(1)}, f32[72,128]{1,0:T(8,128)S(1)}, u32[]{:S(2)}, u32[]{:S(2)}) %collective-permute-start.2) | collective-permute-done | bytes 36896 | tf_op jit(solution)/shard_map/ppermute | solution.py:540
  17.3 1.0 %collective-permute-done.1.refs_1_.z1 = f32[72,128]{1,0:T(8,128)S(1)} collective-permute-done((f32[72,128]{1,0:T(8,128)S(1)}, f32[72,128]{1,0:T(8,128)S(1)}, u32[]{:S(2)}, u32[]{:S(2)}) %collective-permute-start.1) | collective-permute-done | bytes 36896 | tf_op jit(solution)/shard_map/ppermute | solution.py:540
  18.3 0.1 shard_map.39.refs_0_
  18.3 5.4 %collective-permute-start.4 = (f32[72,128]{1,0:T(8,128)S(1)}, f32[72,128]{1,0:T(8,128)S(1)}, u32[]{:S(2)}, u32[]{:S(2)}) collective-permute-start(f32[72,128]{1,0:T(8,128)S(1)} %shard_map.39.refs_0_), channel_id=1, source_target_pairs={{0,56},{8,48},{16,40},{24,32},{32,24},{40,16},{48,8},{56,0},{1,57}... | collective-permute-start | bytes 110600 | tf_op jit(solution)/shard_map/ppermute | solution.py:552
  23.7 1.9 %collective-permute-done.4.z4.refs_1_ = f32[72,128]{1,0:T(8,128)S(1)} collective-permute-done((f32[72,128]{1,0:T(8,128)S(1)}, f32[72,128]{1,0:T(8,128)S(1)}, u32[]{:S(2)}, u32[]{:S(2)}) %collective-permute-start.4) | collective-permute-done | bytes 36896 | tf_op jit(solution)/shard_map/ppermute | solution.py:552
  25.7 0.3 collective-permute-start.7
  26.0 2.6 %collective-permute-start.6 = (f32[72,128]{1,0:T(8,128)S(1)}, f32[72,128]{1,0:T(8,128)S(1)}, u32[]{:S(2)}, u32[]{:S(2)}) collective-permute-start(f32[72,128]{1,0:T(8,128)S(1)} %shard_map.41), channel_id=1, source_target_pairs={{0,128},{64,192},{128,0},{192,64},{1,129},{65,193},{129,1},{193,65... | collective-permute-start | bytes 110600 | tf_op jit(solution)/shard_map/ppermute | solution.py:540
  28.6 2.4 %collective-permute-done.7.y3 = f32[72,128]{1,0:T(8,128)S(1)} collective-permute-done((f32[72,128]{1,0:T(8,128)S(1)}, f32[72,128]{1,0:T(8,128)S(1)}, u32[]{:S(2)}, u32[]{:S(2)}) %collective-permute-start.7) | collective-permute-done | bytes 36896 | tf_op jit(solution)/shard_map/ppermute | solution.py:540
  30.9 0.1 shard_map.40
  31.1 0.4 collective-permute-done.6.y2
  31.5 3.4 %collective-permute-done.5.y1 = f32[72,128]{1,0:T(8,128)S(1)} collective-permute-done((f32[72,128]{1,0:T(8,128)S(1)}, f32[72,128]{1,0:T(8,128)S(1)}, u32[]{:S(2)}, u32[]{:S(2)}) %collective-permute-start.5) | collective-permute-done | bytes 36896 | tf_op jit(solution)/shard_map/ppermute | solution.py:540
  34.9 0.1 shard_map.42
  35.0 0.4 collective-permute-start.8
  35.4 4.0 %collective-permute-start.9 = (f32[4,8,128]{2,1,0:T(8,128)S(1)}, f32[4,8,128]{2,1,0:T(8,128)S(1)}, u32[]{:S(2)}, u32[]{:S(2)}) collective-permute-start(f32[4,8,128]{2,1,0:T(8,128)S(1)} %get-tuple-element.28), channel_id=1, source_target_pairs={{0,2},{1,3},{2,0},{3,1},{4,6},{5,7},{6,4},{7,5},{8,10},{9,11},{10,... | collective-permute-start | bytes 49160 | tf_op jit(solution)/shard_map/ppermute | solution.py:540
  39.4 0.4 collective-permute-start.10
  39.8 0.1 shard_map.44.refs_2_
  39.9 0.1 shard_map.45.refs_3_
  40.0 0.1 shard_map.46.refs_4_
  40.1 0.7 %shard_map.47 = (f32[512,128]{1,0:T(8,128)S(1)}, f32[132,8,128]{2,1,0:T(8,128)S(1)}, f32[2,128,128]{2,1,0:T(8,128)S(1)}) custom-call(f32[4,8,128]{2,1,0:T(8,128)S(1)} %get-tuple-element.36.refs_0_, f32[4,128,128]{2,1,0:T(8,128)S(1)} %get-tuple-element.37.pack.refs_1_, f32[128,128]{1,0:T(8,128)S(1)} %shard_map.44.refs_2_, f32[128,128]{1,0:T(8,128)S(1)} %shard_map.45.refs_3_, ...), custom_call_target="tpu_custom_call" | custom-call | flops 100000 | bytes 1000000 | tf_op jit(solution)/shard_map/pallas_call | solution.py:507
  40.9 0.4 collective-permute-done.9.refs_1_
  41.3 3.1 %collective-permute-done.10.refs_2_ = f32[4,8,128]{2,1,0:T(8,128)S(1)} collective-permute-done((f32[4,8,128]{2,1,0:T(8,128)S(1)}, f32[4,8,128]{2,1,0:T(8,128)S(1)}, u32[]{:S(2)}, u32[]{:S(2)}) %collective-permute-start.10) | collective-permute-done | bytes 16416 | tf_op jit(solution)/shard_map/ppermute | solution.py:540
  44.4 1.8 %shard_map.48 = f32[2,16,3584]{2,1,0:T(8,128)} custom-call(f32[4,8,128]{2,1,0:T(8,128)S(1)} %collective-permute-done.8.refs_0_, f32[4,8,128]{2,1,0:T(8,128)S(1)} %collective-permute-done.9.refs_1_, f32[4,8,128]{2,1,0:T(8,128)S(1)} %collective-permute-done.10.refs_2_, f32[4,128,128]{2,1,0:T(8,128)S(1)} %collective-permute-done.11.pack.refs_3_, ...), custom_call_target="tpu_custom_call" | custom-call | flops 100000 | bytes 1000000 | tf_op jit(solution)/shard_map/pallas_call | solution.py:507
  (8 shorter events, 0.1 us)
Async XLA Ops:
  1.6 37.8 %collective-permute-start.11 = (f32[4,128,128]{2,1,0:T(8,128)S(1)}, f32[4,128,128]{2,1,0:T(8,128)S(1)}, u32[]{:S(2)}, u32[]{:S(2)}) collective-permute-start(f32[4,128,128]{2,1,0:T(8,128)S(1)} %get-tuple-element.33), channel_id=1, source_target_pairs={{0,1},{1,0},{2,3},{3,2},{4,5},{5,4},{6,7},{7,6},{8,9},{9,8},{10,11... | collective-permute-start | bytes 786440 | tf_op jit(solution)/shard_map/ppermute | solution.py:540
  3.2 36.8 %collective-permute-start.12 = (f32[4,128,128]{2,1,0:T(8,128)S(1)}, f32[4,128,128]{2,1,0:T(8,128)S(1)}, u32[]{:S(2)}, u32[]{:S(2)}) collective-permute-start(f32[4,128,128]{2,1,0:T(8,128)S(1)} %get-tuple-element.34), channel_id=1, source_target_pairs={{0,2},{1,3},{2,0},{3,1},{4,6},{5,7},{6,4},{7,5},{8,10},{9,11},{10,... | collective-permute-start | bytes 786440 | tf_op jit(solution)/shard_map/ppermute | solution.py:540
  5.9 34.2 %collective-permute-start.13 = (f32[4,128,128]{2,1,0:T(8,128)S(1)}, f32[4,128,128]{2,1,0:T(8,128)S(1)}, u32[]{:S(2)}, u32[]{:S(2)}) collective-permute-start(f32[4,128,128]{2,1,0:T(8,128)S(1)} %get-tuple-element.35), channel_id=1, source_target_pairs={{0,3},{1,2},{2,1},{3,0},{4,7},{5,6},{6,5},{7,4},{8,11},{9,10},{10,... | collective-permute-start | bytes 786440 | tf_op jit(solution)/shard_map/ppermute | solution.py:540
  6.4 1.2 %collective-permute-start = (f32[72,128]{1,0:T(8,128)S(1)}, f32[72,128]{1,0:T(8,128)S(1)}, u32[]{:S(2)}, u32[]{:S(2)}) collective-permute-start(f32[72,128]{1,0:T(8,128)S(1)} %get-tuple-element.23.refs_0_.own), channel_id=1, source_target_pairs={{0,4},{4,0},{1,5},{5,1},{2,6},{6,2},{3,7},{7,3},{8,12},{12,8},{9,1... | collective-permute-start | bytes 110600 | tf_op jit(solution)/shard_map/ppermute | solution.py:540
  7.6 6.6 %collective-permute-start.3 = (f32[72,128]{1,0:T(8,128)S(1)}, f32[72,128]{1,0:T(8,128)S(1)}, u32[]{:S(2)}, u32[]{:S(2)}) collective-permute-start(f32[72,128]{1,0:T(8,128)S(1)} %shard_map.38.refs_0_), channel_id=1, source_target_pairs={{0,24},{8,16},{16,8},{24,0},{32,56},{40,48},{48,40},{56,32},{1,25}... | collective-permute-start | bytes 110600 | tf_op jit(solution)/shard_map/ppermute | solution.py:540
  12.4 4.9 %collective-permute-start.2 = (f32[72,128]{1,0:T(8,128)S(1)}, f32[72,128]{1,0:T(8,128)S(1)}, u32[]{:S(2)}, u32[]{:S(2)}) collective-permute-start(f32[72,128]{1,0:T(8,128)S(1)} %shard_map.38.refs_0_), channel_id=1, source_target_pairs={{0,16},{8,24},{16,0},{24,8},{32,48},{40,56},{48,32},{56,40},{1,17}... | collective-permute-start | bytes 110600 | tf_op jit(solution)/shard_map/ppermute | solution.py:540
  14.3 4.0 %collective-permute-start.1 = (f32[72,128]{1,0:T(8,128)S(1)}, f32[72,128]{1,0:T(8,128)S(1)}, u32[]{:S(2)}, u32[]{:S(2)}) collective-permute-start(f32[72,128]{1,0:T(8,128)S(1)} %shard_map.38.refs_0_), channel_id=1, source_target_pairs={{0,8},{8,0},{16,24},{24,16},{32,40},{40,32},{48,56},{56,48},{1,9},... | collective-permute-start | bytes 110600 | tf_op jit(solution)/shard_map/ppermute | solution.py:540
  18.3 7.3 %collective-permute-start.4 = (f32[72,128]{1,0:T(8,128)S(1)}, f32[72,128]{1,0:T(8,128)S(1)}, u32[]{:S(2)}, u32[]{:S(2)}) collective-permute-start(f32[72,128]{1,0:T(8,128)S(1)} %shard_map.39.refs_0_), channel_id=1, source_target_pairs={{0,56},{8,48},{16,40},{24,32},{32,24},{40,16},{48,8},{56,0},{1,57}... | collective-permute-start | bytes 110600 | tf_op jit(solution)/shard_map/ppermute | solution.py:552
  25.7 5.3 %collective-permute-start.7 = (f32[72,128]{1,0:T(8,128)S(1)}, f32[72,128]{1,0:T(8,128)S(1)}, u32[]{:S(2)}, u32[]{:S(2)}) collective-permute-start(f32[72,128]{1,0:T(8,128)S(1)} %shard_map.41), channel_id=1, source_target_pairs={{0,192},{64,128},{128,64},{192,0},{1,193},{65,129},{129,65},{193,1... | collective-permute-start | bytes 110600 | tf_op jit(solution)/shard_map/ppermute | solution.py:540
  26.0 5.5 %collective-permute-start.6 = (f32[72,128]{1,0:T(8,128)S(1)}, f32[72,128]{1,0:T(8,128)S(1)}, u32[]{:S(2)}, u32[]{:S(2)}) collective-permute-start(f32[72,128]{1,0:T(8,128)S(1)} %shard_map.41), channel_id=1, source_target_pairs={{0,128},{64,192},{128,0},{192,64},{1,129},{65,193},{129,1},{193,65... | collective-permute-start | bytes 110600 | tf_op jit(solution)/shard_map/ppermute | solution.py:540
  30.9 4.0 %collective-permute-start.5 = (f32[72,128]{1,0:T(8,128)S(1)}, f32[72,128]{1,0:T(8,128)S(1)}, u32[]{:S(2)}, u32[]{:S(2)}) collective-permute-start(f32[72,128]{1,0:T(8,128)S(1)} %shard_map.41), channel_id=1, source_target_pairs={{0,64},{64,0},{128,192},{192,128},{1,65},{65,1},{129,193},{193,129... | collective-permute-start | bytes 110600 | tf_op jit(solution)/shard_map/ppermute | solution.py:540
  35.0 5.9 %collective-permute-start.8 = (f32[4,8,128]{2,1,0:T(8,128)S(1)}, f32[4,8,128]{2,1,0:T(8,128)S(1)}, u32[]{:S(2)}, u32[]{:S(2)}) collective-permute-start(f32[4,8,128]{2,1,0:T(8,128)S(1)} %get-tuple-element.27), channel_id=1, source_target_pairs={{0,1},{1,0},{2,3},{3,2},{4,5},{5,4},{6,7},{7,6},{8,9},{9,8},{10,11... | collective-permute-start | bytes 49160 | tf_op jit(solution)/shard_map/ppermute | solution.py:540
  35.4 5.9 %collective-permute-start.9 = (f32[4,8,128]{2,1,0:T(8,128)S(1)}, f32[4,8,128]{2,1,0:T(8,128)S(1)}, u32[]{:S(2)}, u32[]{:S(2)}) collective-permute-start(f32[4,8,128]{2,1,0:T(8,128)S(1)} %get-tuple-element.28), channel_id=1, source_target_pairs={{0,2},{1,3},{2,0},{3,1},{4,6},{5,7},{6,4},{7,5},{8,10},{9,11},{10,... | collective-permute-start | bytes 49160 | tf_op jit(solution)/shard_map/ppermute | solution.py:540
  39.4 5.0 %collective-permute-start.10 = (f32[4,8,128]{2,1,0:T(8,128)S(1)}, f32[4,8,128]{2,1,0:T(8,128)S(1)}, u32[]{:S(2)}, u32[]{:S(2)}) collective-permute-start(f32[4,8,128]{2,1,0:T(8,128)S(1)} %get-tuple-element.29), channel_id=1, source_target_pairs={{0,3},{1,2},{2,1},{3,0},{4,7},{5,6},{6,5},{7,4},{8,11},{9,10},{10,... | collective-permute-start | bytes 49160 | tf_op jit(solution)/shard_map/ppermute | solution.py:540
